TPU v7x, 256 devices: a whole 4x4x8 slice. The times are simulated.
256 devices in a mesh: dp: 4 (over x), space: 64 (over z, y, core).
Axes of the slice: x: 4, y: 4, z: 8, core: 2. Of those that a mesh axis runs over, the one named last changes fastest.
Arguments:
- fields: bfloat16 [4, 32, 6144, 128], P('dp', None, 'space'), may hold values from -6 to 6
- land_mask: int32 [6144, 128], P('space'), may hold values from 0 to 1, as said below
- land_frac: float32 [6144, 128], P('space'), may hold values from 0.05 to 1
- owner_map: int32 [12288], replicated, may hold values from 0 to 12287, as said below
- targets: float32 [4, 14, 12288], P('dp', None, 'space'), may hold values from -3 to 3
- conv_weight: bfloat16 [3, 3, 32, 128], replicated, may hold values from -0.375 to 0.375
- conv_bias: float32 [128], replicated, may hold values from -3 to 3
- mix_weight: bfloat16 [128, 128], replicated, may hold values from -0.5 to 0.5
- mix_bias: float32 [128], replicated, may hold values from -3 to 3
- out_weight: bfloat16 [128, 14], replicated, may hold values from -0.5 to 0.5
- out_bias: float32 [14], replicated, may hold values from -3 to 3
Outputs:
- coarse_pred: float32 [4, 14, 12288], P('dp', None, 'space')
- conv_grad: float32 [3, 3, 32, 128], replicated
- conv_bias_grad: float32 [128], replicated
- mix_grad: float32 [128, 128], replicated
- mix_bias_grad: float32 [128], replicated
- out_grad: float32 [128, 14], replicated
- out_bias_grad: float32 [14], replicated
- loss: float32 [], replicated
Inputs may be any that keep to these rules, and one draw needn't show every extreme that they name: A permutation. Coarse cell g is owned by index owner_map[g] // 192 of space, at local place owner_map[g] % 192; the 192 coarse cells of every strip go to every owner exactly 3 at a time. `land_mask`: 1 marks land.
All inputs are finite; a program needn't handle non-finite values.
Results may differ from a plain program's by a relative error of at most 0.00039.
Values may be sent and summed in bfloat16 or wider, within the bound.
A program may use at most 128 MiB of HBM per device.

v0:
```python
import math
import jax
import jax.numpy as jnp
from jax import lax
from jax.sharding import PartitionSpec as P

SIDE = 8
CUBIC = 0.044715
ROOT_TWO_PI = math.sqrt(2.0 / math.pi)


def padded_2(block, sides, width):
    for axis, dim in sides:
        count = lax.axis_size(axis)
        forward = [(i, i + 1) for i in range(count - 1)]
        backward = [(target, source) for source, target in forward]
        low = lax.ppermute(
            lax.slice_in_dim(block, block.shape[dim] - width, None, axis=dim), axis, forward
        )
        high = lax.ppermute(lax.slice_in_dim(block, 0, width, axis=dim), axis, backward)
        block = jnp.concatenate([low, block, high], axis=dim)
    return block


def gelu_pair(pre):
    inner = ROOT_TWO_PI * (pre + CUBIC * pre * pre * pre)
    tanh_value = jnp.tanh(inner)
    value = 0.5 * pre * (1.0 + tanh_value)
    slope = 0.5 * (1.0 + tanh_value) + 0.5 * pre * (1.0 - tanh_value * tanh_value) * ROOT_TWO_PI * (
        1.0 + 3.0 * CUBIC * pre * pre
    )
    return (value, slope)


def product(form, left, right):
    return jnp.einsum(form, left, right, preferred_element_type=jnp.float32)


def block_sums(values, side):
    leading = values.shape[:-2]
    height, breadth = (values.shape[-2], values.shape[-1])
    shaped = values.reshape(leading + (height // side, side, breadth // side, side))
    return jnp.sum(shaped, axis=(-3, -1)).reshape(leading + (height // side * (breadth // side),))


def forward_tile(padded, conv_weight, conv_bias, mix_weight, mix_bias, out_weight, out_bias):
    height = padded.shape[2] - 2
    breadth = padded.shape[3] - 2
    pieces = [
        padded[:, :, row_shift : row_shift + height, col_shift : col_shift + breadth]
        for row_shift in range(3)
        for col_shift in range(3)
    ]
    stacked = jnp.concatenate(pieces, axis=1)
    flat_weight = conv_weight.reshape(-1, conv_weight.shape[3])
    pre_one = product("mkrc,kh->mrch", stacked, flat_weight) + conv_bias
    value_one, slope_one = gelu_pair(pre_one)
    hidden_one = value_one.astype(jnp.bfloat16)
    pre_two = product("mrch,hg->mrcg", hidden_one, mix_weight) + mix_bias
    value_two, slope_two = gelu_pair(pre_two)
    hidden_two = value_two.astype(jnp.bfloat16)
    raw = product("mrch,hp->mprc", hidden_two, out_weight) + out_bias[None, :, None, None]
    return (stacked, slope_one, hidden_one, slope_two, hidden_two, raw)


def backward_tile(
    stacked,
    slope_one,
    hidden_one,
    slope_two,
    hidden_two,
    raw,
    weight_map,
    d_block,
    mix_weight,
    out_weight,
    side,
):
    members, pools = (d_block.shape[0], d_block.shape[1])
    height, breadth = weight_map.shape
    d_cells = d_block.reshape(members, pools, height // side, breadth // side)
    d_cells = jnp.repeat(jnp.repeat(d_cells, side, axis=2), side, axis=3)
    d_raw = (d_cells * weight_map * jax.nn.sigmoid(raw)).astype(jnp.bfloat16)
    out_grad = product("mrch,mprc->hp", hidden_two, d_raw)
    out_bias_grad = jnp.sum(d_raw.astype(jnp.float32), axis=(0, 2, 3))
    d_two = (product("mprc,hp->mrch", d_raw, out_weight) * slope_two).astype(jnp.bfloat16)
    mix_grad = product("mrch,mrcg->hg", hidden_one, d_two)
    mix_bias_grad = jnp.sum(d_two.astype(jnp.float32), axis=(0, 1, 2))
    d_one = (product("mrcg,hg->mrch", d_two, mix_weight) * slope_one).astype(jnp.bfloat16)
    conv_grad = product("mkrc,mrch->kh", stacked, d_one)
    conv_bias_grad = jnp.sum(d_one.astype(jnp.float32), axis=(0, 1, 2))
    return (conv_grad, conv_bias_grad, mix_grad, mix_bias_grad, out_grad, out_bias_grad)


def route_tables(owner_map, position, peers, blocks):
    capacity = blocks // peers
    serial = jnp.arange(blocks, dtype=jnp.int32)
    owned = lax.dynamic_slice_in_dim(owner_map, position * blocks, blocks)
    target = owned // blocks
    earlier = serial[None, :] < serial[:, None]
    ranking = jnp.sum((target[None, :] == target[:, None]) & earlier, axis=1)
    send_slot = target * capacity + ranking
    slot_block = jnp.zeros((blocks,), jnp.int32).at[send_slot].set(serial)
    count_all = owner_map.shape[0]
    inverse = (
        jnp.zeros((count_all,), jnp.int32).at[owner_map].set(jnp.arange(count_all, dtype=jnp.int32))
    )
    mine_list = lax.dynamic_slice_in_dim(inverse, position * blocks, blocks)
    source = mine_list // blocks
    within = mine_list % blocks
    source_rows = owner_map.reshape(peers, blocks)[source] // blocks
    before = serial[None, :] < within[:, None]
    home_rank = jnp.sum((source_rows == position) & before, axis=1)
    home_slot = source * capacity + home_rank
    return (owned, send_slot, slot_block, home_slot, mine_list)


def on_device(
    fields,
    land_mask,
    land_frac,
    owner_map,
    targets,
    conv_weight,
    conv_bias,
    mix_weight,
    mix_bias,
    out_weight,
    out_bias,
):
    peers = lax.axis_size("space")
    position = lax.axis_index("space")
    members = fields.shape[0]
    pools = out_weight.shape[1]
    tile_rows = fields.shape[2]
    tile_cols = fields.shape[3]
    blocks = tile_rows // SIDE * (tile_cols // SIDE)
    capacity = blocks // peers
    extended = padded_2(fields, (("space", 2),), 1)
    padded = jnp.pad(extended, ((0, 0), (0, 0), (0, 0), (1, 1)))
    outputs = forward_tile(
        padded, conv_weight, conv_bias, mix_weight, mix_bias, out_weight, out_bias
    )
    weight_map = land_frac * land_mask.astype(jnp.float32)
    density = jax.nn.softplus(outputs[5]) * weight_map
    owned, send_slot, slot_block, home_slot, mine_list = route_tables(
        owner_map, position, peers, blocks
    )
    strip_values = block_sums(density, SIDE)
    strip_weights = block_sums(weight_map, SIDE)
    got_values, got_weights = (
        lax.all_to_all(
            strip_values[:, :, slot_block].reshape(members, pools, peers, capacity),
            "space",
            split_axis=2,
            concat_axis=2,
            tiled=True,
        ),
        lax.all_to_all(
            strip_weights[slot_block].reshape(1, 1, peers, capacity),
            "space",
            split_axis=2,
            concat_axis=2,
            tiled=True,
        ),
    )
    coarse_sum = got_values.reshape(members, pools, blocks)[:, :, home_slot]
    coarse_weight = got_weights.reshape(blocks)[home_slot]
    denom = jnp.maximum(coarse_weight, 1.0)
    coarse_pred = coarse_sum / denom
    residual = coarse_pred - targets
    count_all = members * lax.axis_size("dp") * pools * owner_map.shape[0]
    d_coarse = residual / (math.sqrt(count_all) * denom)
    serial = jnp.arange(blocks, dtype=jnp.int32)
    back_order = jnp.zeros((blocks,), jnp.int32).at[home_slot].set(serial)
    returned = lax.all_to_all(
        d_coarse[:, :, back_order].reshape(members, pools, peers, capacity),
        "space",
        split_axis=2,
        concat_axis=2,
        tiled=True,
    )
    d_block = returned.reshape(members, pools, blocks)[:, :, send_slot]
    grads = backward_tile(*outputs, weight_map, d_block, mix_weight, out_weight, SIDE)
    squares = jnp.sum(residual * residual)
    conv_grad, conv_bias_grad, mix_grad, mix_bias_grad, out_grad, out_bias_grad, total = lax.psum(
        (grads[0], grads[1], grads[2], grads[3], grads[4], grads[5], squares), ("dp", "space")
    )
    loss = 0.5 * total / count_all
    conv_grad = conv_grad.reshape(conv_weight.shape)
    return (
        coarse_pred,
        conv_grad,
        conv_bias_grad,
        mix_grad,
        mix_bias_grad,
        out_grad,
        out_bias_grad,
        loss,
    )


def solution(mesh):
    placed = (
        P("dp", None, "space", None),
        P("space", None),
        P("space", None),
        P(),
        P("dp", None, "space"),
        P(),
        P(),
        P(),
        P(),
        P(),
        P(),
    )
    return jax.shard_map(
        on_device,
        mesh=mesh,
        in_specs=placed,
        out_specs=(P("dp", None, "space"), P(), P(), P(), P(), P(), P(), P()),
        check_vma=False,
    )
```

profile of v0, /device:TPU:2, one launch (start us, length us, event | category | flops | bytes accessed | tf_op | source)
XLA Modules:
  0.0 444.0 jit_solution(1950870400691555517)
XLA Ops:
  7.2 1.5 copy.71
  8.7 1.7 collective-permute-start
  12.6 45.4 %scatter_custom_fusion.1 = s32[12288]{0:T(1024)S(1)} fusion(s32[12288]{0:T(1024)S(1)} %compare_select_fusion.1, s32[12288]{0:T(1024)S(1)} %iota.16, s32[]{:T(128)} %constant.30.clone.1), kind=kCustom, calls=%fused_computation.83 | custom fusion | bytes 49156 | tf_op jit(solution)/shard_map/scatter | solution.py:106
  61.7 1.6 gather_fusion.3
  64.1 15.3 %all-to-all-start.1 = ((f32[1,1,64,3]{3,1,0,2:T(1,128)}), f32[1,1,64,3]{3,1,0,2:T(1,128)S(1)}, u32[]{:S(2)}, u32[]{:S(2)}) async-start(f32[1,1,64,3]{3,1,0,2:T(1,128)} %bitcast.12), calls=%async_computation.1 | async-start | bytes 65536 | tf_op jit(solution)/shard_map/all_to_all | solution.py:159
  81.5 1.4 scatter_custom_fusion.2
  83.0 6.0 %all-to-all-done.1 = f32[1,1,64,3]{3,1,0,2:T(1,128)S(1)} async-done(((f32[1,1,64,3]{3,1,0,2:T(1,128)}), f32[1,1,64,3]{3,1,0,2:T(1,128)S(1)}, u32[]{:S(2)}, u32[]{:S(2)}) %all-to-all-start.1) | async-done | bytes 800 | tf_op jit(solution)/shard_map/all_to_all | solution.py:159
  90.3 1.6 gather_fusion.4
  95.3 2.9 copy-done.1
  98.2 2.7 fusion.2
  101.0 6.2 %multiply_convert_fusion = (bf16[96,128,128]{2,1,0:T(8,128)(2,1)S(1)}, f32[96,128,128]{2,1,0:T(8,128)}) fusion(f32[128]{0:T(128)S(1)} %copy-done.9, bf16[128,128]{1,0:T(8,128)(2,1)S(1)} %copy-done.8, f32[96,128,128]{2,1,0:T(8,128)S(1)} %fusion.2, f32[128]{0:T(128)S(1)} %copy-done.10), kind=kOutput, calls=%fused_computation.34 | convolution fusion | flops 434110464 | bytes 15762432 | tf_op jit(solution)/shard_map/mrch,hg->mrcg/dot_general | solution.py:36
  107.1 1.8 fusion.25
  110.0 8.5 %reshape.223 = f32[14,12,8,16,8]{4,3,2,1,0:T(8,128)} reshape(f32[14,96,128]{2,1,0:T(8,128)} %copy.77) | data formatting | bytes 1376256 | tf_op jit(solution)/shard_map/reshape | solution.py:42
  118.6 5.6 %reduce_sum.72 = f32[14,12,16]{2,1,0:T(8,128)} reduce(f32[14,12,8,16,8]{4,3,2,1,0:T(8,128)} %reshape.223, f32[]{:T(128)} %constant.29.clone.1), dimensions={2,4}, to_apply=%region_0.1 | reduce | flops 169344 | bytes 698884 | tf_op jit(solution)/shard_map/reduce_sum | solution.py:43
  126.5 4.8 %all-to-all-start = ((f32[1,14,64,3]{1,0,3,2:T(1,128)}), f32[1,14,64,3]{1,0,3,2:T(1,128)S(1)}, u32[]{:S(2)}, u32[]{:S(2)}) async-start(f32[1,14,64,3]{1,0,3,2:T(1,128)} %bitcast.78), calls=%async_computation | async-start | bytes 196608 | tf_op jit(solution)/shard_map/all_to_all | solution.py:152
  131.3 10.3 %all-to-all-done = f32[1,14,64,3]{1,0,3,2:T(1,128)S(1)} async-done(((f32[1,14,64,3]{1,0,3,2:T(1,128)}), f32[1,14,64,3]{1,0,3,2:T(1,128)S(1)}, u32[]{:S(2)}, u32[]{:S(2)}) %all-to-all-start) | async-done | bytes 10784 | tf_op jit(solution)/shard_map/all_to_all | solution.py:152
  143.0 1.6 multiply_reduce_fusion
  145.3 2.2 gather_fusion.5
  147.5 4.6 %all-to-all-start.2 = ((f32[1,14,64,3]{1,0,3,2:T(1,128)}), f32[1,14,64,3]{1,0,3,2:T(1,128)S(1)}, u32[]{:S(2)}, u32[]{:S(2)}) async-start(f32[1,14,64,3]{1,0,3,2:T(1,128)} %bitcast.77), calls=%async_computation.2 | async-start | bytes 196608 | tf_op jit(solution)/shard_map/all_to_all | solution.py:176
  152.8 9.8 %all-to-all-done.2 = f32[1,14,64,3]{1,0,3,2:T(1,128)S(1)} async-done(((f32[1,14,64,3]{1,0,3,2:T(1,128)}), f32[1,14,64,3]{1,0,3,2:T(1,128)S(1)}, u32[]{:S(2)}, u32[]{:S(2)}) %all-to-all-start.2) | async-done | bytes 10784 | tf_op jit(solution)/shard_map/all_to_all | solution.py:176
  165.9 1.3 copy.84
  168.2 2.5 copy.85
  170.7 1.9 convert_reduce_fusion.2
  172.6 6.8 %convert_reduce_fusion = (f32[128]{0:T(128)S(1)}, bf16[96,128,128]{2,1,0:T(8,128)(2,1)S(1)}) fusion(f32[96,128,128]{2,1,0:T(8,128)} %get-tuple-element.67, f32[128]{0:T(128)S(1)} %copy-done.9, bf16[14,96,128]{2,0,1:T(8,128)(2,1)S(1)} %get-tuple-element.58, bf16[128,14]{0,1:T(8,128)(2,1)S(1)} %copy-done.6), kind=kOutput, calls=%fused_computation.32 | convolution fusion | flops 78643072 | bytes 9785856 | tf_op jit(solution)/shard_map/mprc,hp->mrch/dot_general | solution.py:36
  179.5 4.7 %convert_reduce_fusion.1 = (f32[128]{0:T(128)S(1)}, bf16[96,128,128]{2,1,0:T(8,128)(2,1)S(1)}) fusion(f32[96,128,128]{2,1,0:T(8,128)S(1)} %bitcast.72, f32[128]{0:T(128)S(1)} %copy-done.10, bf16[96,128,128]{2,1,0:T(8,128)(2,1)S(1)} %get-tuple-element.73, bf16[128,128]{1,0:T(8,128)(2,1)S(1)} %copy-done.8), kind=kOutput, calls=%fused_computation.33 | convolution fusion | flops 437256064 | bytes 12616704 | tf_op jit(solution)/shard_map/mrcg,hg->mrch/dot_general | solution.py:36
  184.3 3.2 convolution_bitcast_fusion
  187.5 2.6 fusion
  190.1 1.5 convolution_bitcast_fusion.1
  191.6 73.9 %all-reduce.1 = (f32[128]{0:T(128)}, f32[128]{0:T(128)}, f32[128,14]{0,1:T(8,128)}, f32[14]{0:T(128)}, f32[]{:T(128)}) all-reduce(f32[128]{0:T(128)S(1)} %get-tuple-element.70, f32[128]{0:T(128)S(1)} %get-tuple-element.72, f32[128,14]{0,1:T(8,128)S(1)} %convolution_bitcast_fusion.1, ...), channel_id=1, replica_groups=mesh['dp'=4,'space'=64] {'dp','space'}, use_global_device_ids=true, to_apply=%region_9.10 | all-reduce | flops 2063 | bytes 16504 | tf_op jit(solution)/shard_map/psum | solution.py:186
  266.2 166.8 %all-reduce.5.cloned.1.call-done = (f32[3,3,32,128]{3,2,1,0:T(8,128)}, f32[128,128]{1,0:T(8,128)}) async-done(((f32[3,3,32,128]{3,2,1,0:T(8,128)}, f32[128,128]{1,0:T(8,128)}), (f32[3,3,32,128]{3,2,1,0:T(8,128)}, f32[128,128]{1,0:T(8,128)})) %all-reduce.5.cloned.1.call-update) | async-done | bytes 213008 | tf_op jit(solution)/shard_map/psum | solution.py:186
  433.0 1.6 copy.100
  434.5 1.5 copy.101
  (86 shorter events, 23.8 us)
Async XLA Ops:
  7.2 88.1 %copy-start = (bf16[3,3,32,128]{3,2,1,0:T(8,128)(2,1)S(1)}, bf16[3,3,32,128]{3,2,1,0:T(8,128)(2,1)}, u32[]{:S(2)}) copy-start(bf16[3,3,32,128]{3,2,1,0:T(8,128)(2,1)} %param.16) | copy-start | bytes 221188
  7.2 75.7 %copy-start.5 = (f32[1,14,192]{2,0,1:T(1,128)S(1)}, f32[1,14,192]{2,0,1:T(1,128)}, u32[]{:S(2)}) copy-start(f32[1,14,192]{2,0,1:T(1,128)} %param.15) | copy-start | bytes 32260
  8.7 83.3 %collective-permute-start = (bf16[1,32,1,128]{3,1,2,0:T(8,128)(2,1)S(1)}, bf16[1,32,1,128]{3,1,2,0:T(8,128)(2,1)S(1)}, u32[]{:S(2)}, u32[]{:S(2)}) collective-permute-start(bf16[1,32,1,128]{3,1,2,0:T(8,128)(2,1)S(1)} %get-tuple-element.61), channel_id=1, source_target_pairs={{0,1},{1,2},{2,3},{3,4},{4,5},{5,6},{6,7},{7,8},{8,9},{9,10},{10,1... | collective-permute-start | bytes 24584 | tf_op jit(solution)/shard_map/ppermute | solution.py:17
  10.4 81.5 %collective-permute-start.1 = (bf16[1,32,1,128]{3,1,2,0:T(8,128)(2,1)S(1)}, bf16[1,32,1,128]{3,1,2,0:T(8,128)(2,1)S(1)}, u32[]{:S(2)}, u32[]{:S(2)}) collective-permute-start(bf16[1,32,1,128]{3,1,2,0:T(8,128)(2,1)S(1)} %get-tuple-element.62), channel_id=1, source_target_pairs={{1,0},{2,1},{3,2},{4,3},{5,4},{6,5},{7,6},{8,7},{9,8},{10,9},{11,1... | collective-permute-start | bytes 24584 | tf_op jit(solution)/shard_map/ppermute | solution.py:20
  63.3 30.4 %copy-start.3 = (bf16[1,32,96,128]{3,2,1,0:T(8,128)(2,1)S(1)}, bf16[1,32,96,128]{3,2,1,0:T(8,128)(2,1)}, u32[]{:S(2)}) copy-start(bf16[1,32,96,128]{3,2,1,0:T(8,128)(2,1)} %param.11) | copy-start | bytes 2359300
  64.1 24.9 %all-to-all-start.1 = ((f32[1,1,64,3]{3,1,0,2:T(1,128)}), f32[1,1,64,3]{3,1,0,2:T(1,128)S(1)}, u32[]{:S(2)}, u32[]{:S(2)}) async-start(f32[1,1,64,3]{3,1,0,2:T(1,128)} %bitcast.12), calls=%async_computation.1 | async-start | bytes 65536 | tf_op jit(solution)/shard_map/all_to_all | solution.py:159
  95.3 2.9 copy-start.1
  98.2 2.8 copy-start.8
  98.2 2.8 copy-start.9
  98.2 2.8 copy-start.10
  100.9 6.2 %copy-start.2 = (f32[96,128,128]{2,1,0:T(8,128)}, f32[96,128,128]{2,1,0:T(8,128)S(1)}, u32[]{:S(2)}) copy-start(f32[96,128,128]{2,1,0:T(8,128)S(1)} %fusion.2) | copy-start | bytes 18874372
  100.9 6.2 %copy-start.6 = (bf16[128,14]{0,1:T(8,128)(2,1)S(1)}, bf16[128,14]{0,1:T(8,128)(2,1)}, u32[]{:S(2)}) copy-start(bf16[128,14]{0,1:T(8,128)(2,1)} %param.20) | copy-start | bytes 10756
  101.0 6.2 %copy-start.7 = (f32[14]{0:T(128)S(1)}, f32[14]{0:T(128)}, u32[]{:S(2)}) copy-start(f32[14]{0:T(128)} %param.21) | copy-start | bytes 172
  126.5 15.2 %all-to-all-start = ((f32[1,14,64,3]{1,0,3,2:T(1,128)}), f32[1,14,64,3]{1,0,3,2:T(1,128)S(1)}, u32[]{:S(2)}, u32[]{:S(2)}) async-start(f32[1,14,64,3]{1,0,3,2:T(1,128)} %bitcast.78), calls=%async_computation | async-start | bytes 196608 | tf_op jit(solution)/shard_map/all_to_all | solution.py:152
  147.5 15.1 %all-to-all-start.2 = ((f32[1,14,64,3]{1,0,3,2:T(1,128)}), f32[1,14,64,3]{1,0,3,2:T(1,128)S(1)}, u32[]{:S(2)}, u32[]{:S(2)}) async-start(f32[1,14,64,3]{1,0,3,2:T(1,128)} %bitcast.77), calls=%async_computation.2 | async-start | bytes 196608 | tf_op jit(solution)/shard_map/all_to_all | solution.py:176
  152.0 280.9 %all-reduce.5.cloned.1.call-start = ((), (), s32[]{:S(2)}) async-start(), calls=%async_computation.3 | async-start | bytes 425984 | tf_op jit(solution)/shard_map/psum | solution.py:186
  170.7 8.8 %slice-start.2 = ((s8[6291456]{0:T(1024)(128)(4,1)}), s8[4194304]{0:T(1024)(128)(4,1)S(1)}, s32[]{:S(2)}) async-start(s8[6291456]{0:T(1024)(128)(4,1)} %bitcast.71), calls=%async_computation.6 | async-start | bytes 8388608
  172.6 6.9 %copy-start.4 = (bf16[14,96,128]{2,0,1:T(8,128)(2,1)}, bf16[14,96,128]{2,0,1:T(8,128)(2,1)S(1)}, u32[]{:S(2)}) copy-start(bf16[14,96,128]{2,0,1:T(8,128)(2,1)S(1)} %get-tuple-element.58) | copy-start | bytes 1032196
  172.6 6.9 %slice-start.3 = ((s8[6291456]{0:T(1024)(128)(4,1)}), s8[2097152]{0:T(1024)(128)(4,1)S(1)}, s32[]{:S(2)}) async-start(s8[6291456]{0:T(1024)(128)(4,1)} %bitcast.71), calls=%async_computation.7 | async-start | bytes 4194304
  172.6 14.8 %slice-start = ((s8[7077888]{0:T(1024)(128)(4,1)}), s8[4194304]{0:T(1024)(128)(4,1)S(1)}, s32[]{:S(2)}) async-start(s8[7077888]{0:T(1024)(128)(4,1)} %bitcast.69), calls=%async_computation.4 | async-start | bytes 8388608
  179.5 7.9 %slice-start.1 = ((s8[7077888]{0:T(1024)(128)(4,1)}), s8[2883584]{0:T(1024)(128)(4,1)S(1)}, s32[]{:S(2)}) async-start(s8[7077888]{0:T(1024)(128)(4,1)} %bitcast.69), calls=%async_computation.5 | async-start | bytes 5767168
Sparse Core Ops, SparseCore 0:
  190.2 242.6 all-reduce.4
where the time goes:
time: 445 us; the launch traced here: 444 us
  waiting for transfers between devices  193 us (43%)
  local copies, waits for them, and re-layouts  88.8 us (20%)
  blocking collectives  73.9 us (17%)
  matrix products  29.7 us (7%)
  starting transfers between devices  27.8 us (6%)
  between operations  16.3 us (4%)
  other arithmetic  14.7 us (3%)
    psum x1, waiting for transfers between devices, on_device(): lax.psum((grads[0], grads[1], grads[2], grads[3], grads[4], grads[5], squ...  167 us
    psum x1, blocking collectives, on_device(): lax.psum((grads[0], grads[1], grads[2], grads[3], grads[4], grads[5], squ...  73.9 us
    scatter x1, local copies, waits for them, and re-layouts, route_tables(): jnp.zeros((count_all,), jnp.int32).at[owner_map]  45.4 us
    dot_general x8, matrix products, product(): return jnp.einsum(form, left, right, preferred_element_type=jnp.float32)  29.7 us
    all_to_all x1, starting transfers between devices, on_device(): lax.all_to_all(strip_weights[slot_block].reshape(1, 1, peers, capacity),...  15.3 us
    all_to_all x1, waiting for transfers between devices, on_device(): lax.all_to_all(strip_values[:, :, slot_block].reshape(members, pools, pee...  10.3 us
    unnamed x41, local copies, waits for them, and re-layouts  10 us
    all_to_all x1, waiting for transfers between devices, on_device(): lax.all_to_all(d_coarse[:, :, back_order].reshape(members, pools, peers,...  9.81 us
  transfers between devices with their start and end apart: 6, of which 4 were waited for; matrix products, arithmetic and copies ran while one was open for 14% of the time, Pallas kernels for 0%

commit v1 on v0

--- a/solution.py
+++ b/solution.py
@@ -184,7 +184,8 @@
     grads = backward_tile(*outputs, weight_map, d_block, mix_weight, out_weight, SIDE)
     squares = jnp.sum(residual * residual)
     conv_grad, conv_bias_grad, mix_grad, mix_bias_grad, out_grad, out_bias_grad, total = lax.psum(
-        (grads[0], grads[1], grads[2], grads[3], grads[4], grads[5], squares), ("dp", "space")
+        lax.psum((grads[0], grads[1], grads[2], grads[3], grads[4], grads[5], squares), "space"),
+        "dp",
     )
     loss = 0.5 * total / count_all
     conv_grad = conv_grad.reshape(conv_weight.shape)

time: 445 us -> 639 us (1.44)
  blocking collectives: 73.9 us -> 263 us
    psum x1, blocking collectives: 73.9 us -> 248 us  [on_device(): lax.psum((grads[0], grads[1], grads[2], grads[3], grads[4], grads[5], squ...]
    psum x0 -> x1, blocking collectives: none -> 15.1 us  [on_device(): lax.psum(lax.psum((grads[0], grads[1], grads[2], grads[3], grads[4], grad...]
  transfers between devices with their start and end apart: 6 -> 7, of which waited for: 4 -> 4; matrix products, arithmetic and copies ran while one was open for 14% -> 10% of each run, Pallas kernels for 0% -> 0%
where the time goes in v1:
time: 639 us; the launch traced here: 637 us
  blocking collectives  263 us (41%)
  waiting for transfers between devices  194 us (30%)
  local copies, waits for them, and re-layouts  91.9 us (14%)
  matrix products  29.7 us (5%)
  starting transfers between devices  27.8 us (4%)
  between operations  16.3 us (3%)
  other arithmetic  14.7 us (2%)
    psum x1, blocking collectives, on_device(): lax.psum((grads[0], grads[1], grads[2], grads[3], grads[4], grads[5], squ...  248 us
    psum x1, waiting for transfers between devices, on_device(): lax.psum((grads[0], grads[1], grads[2], grads[3], grads[4], grads[5], squ...  167 us
    scatter x1, local copies, waits for them, and re-layouts, route_tables(): jnp.zeros((count_all,), jnp.int32).at[owner_map]  45.4 us
    dot_general x8, matrix products, product(): return jnp.einsum(form, left, right, preferred_element_type=jnp.float32)  29.7 us
    all_to_all x1, starting transfers between devices, on_device(): lax.all_to_all(strip_weights[slot_block].reshape(1, 1, peers, capacity),...  15.3 us
    psum x1, blocking collectives, on_device(): lax.psum(lax.psum((grads[0], grads[1], grads[2], grads[3], grads[4], grad...  15.1 us
  transfers between devices with their start and end apart: 7, of which 4 were waited for; matrix products, arithmetic and copies ran while one was open for 10% of the time, Pallas kernels for 0%

profile of v1, /device:TPU:2, one launch (start us, length us, event | category | flops | bytes accessed | tf_op | source)
XLA Modules:
  0.0 637.2 jit_solution(17038623486909214811)
XLA Ops:
  8.7 1.7 collective-permute-start
  12.6 45.4 %scatter_custom_fusion.1 = s32[12288]{0:T(1024)S(1)} fusion(s32[12288]{0:T(1024)S(1)} %compare_select_fusion.1, s32[12288]{0:T(1024)S(1)} %iota.16, s32[]{:T(128)} %constant.30.clone.1), kind=kCustom, calls=%fused_computation.84 | custom fusion | bytes 49156 | tf_op jit(solution)/shard_map/scatter | solution.py:106
  61.7 1.6 gather_fusion.3
  64.1 15.3 %all-to-all-start.1 = ((f32[1,1,64,3]{3,1,0,2:T(1,128)}), f32[1,1,64,3]{3,1,0,2:T(1,128)S(1)}, u32[]{:S(2)}, u32[]{:S(2)}) async-start(f32[1,1,64,3]{3,1,0,2:T(1,128)} %bitcast.12), calls=%async_computation.1 | async-start | bytes 65536 | tf_op jit(solution)/shard_map/all_to_all | solution.py:159
  83.0 6.0 all-to-all-done.1
  90.3 1.6 gather_fusion.4
  95.3 2.9 copy-done.1
  98.2 2.7 fusion.2
  101.0 6.2 multiply_convert_fusion
  107.1 1.8 fusion.28
  110.0 8.5 %reshape.223 = f32[14,12,8,16,8]{4,3,2,1,0:T(8,128)} reshape(f32[14,96,128]{2,1,0:T(8,128)} %copy.77) | data formatting | bytes 1376256 | tf_op jit(solution)/shard_map/reshape | solution.py:42
  118.6 5.6 reduce_sum.72
  126.5 4.8 all-to-all-start
  131.3 10.3 %all-to-all-done = f32[1,14,64,3]{1,0,3,2:T(1,128)S(1)} async-done(((f32[1,14,64,3]{1,0,3,2:T(1,128)}), f32[1,14,64,3]{1,0,3,2:T(1,128)S(1)}, u32[]{:S(2)}, u32[]{:S(2)}) %all-to-all-start) | async-done | bytes 10784 | tf_op jit(solution)/shard_map/all_to_all | solution.py:152
  143.0 1.6 multiply_reduce_fusion
  145.3 2.2 gather_fusion.5
  147.5 4.6 all-to-all-start.2
  152.1 10.5 %all-to-all-done.2 = f32[1,14,64,3]{1,0,3,2:T(1,128)S(1)} async-done(((f32[1,14,64,3]{1,0,3,2:T(1,128)}), f32[1,14,64,3]{1,0,3,2:T(1,128)S(1)}, u32[]{:S(2)}, u32[]{:S(2)}) %all-to-all-start.2) | async-done | bytes 10784 | tf_op jit(solution)/shard_map/all_to_all | solution.py:176
  163.9 1.7 copy.83
  165.6 1.8 broadcast_bitcast_fusion.1
  167.4 2.0 copy.84
  169.4 1.9 broadcast_bitcast_fusion
  171.3 2.5 copy.85
  173.8 1.9 convert_reduce_fusion.2
  175.7 6.8 %convert_reduce_fusion = (f32[128]{0:T(128)S(1)}, bf16[96,128,128]{2,1,0:T(8,128)(2,1)S(1)}) fusion(f32[96,128,128]{2,1,0:T(8,128)} %get-tuple-element.74, f32[128]{0:T(128)S(1)} %copy-done.9, bf16[14,96,128]{2,0,1:T(8,128)(2,1)S(1)} %get-tuple-element.65, bf16[128,14]{0,1:T(8,128)(2,1)S(1)} %copy-done.6), kind=kOutput, calls=%fused_computation.32 | convolution fusion | flops 78643072 | bytes 9785856 | tf_op jit(solution)/shard_map/mprc,hp->mrch/dot_general | solution.py:36
  182.6 4.7 convert_reduce_fusion.1
  187.3 3.2 convolution_bitcast_fusion
  190.5 2.6 fusion.25
  193.9 167.1 %all-reduce.8.cloned.1.call-done = (f32[288,128]{1,0:T(8,128)}, f32[128,128]{1,0:T(8,128)}) async-done(((f32[288,128]{1,0:T(8,128)}, f32[128,128]{1,0:T(8,128)}), (f32[288,128]{1,0:T(8,128)}, f32[128,128]{1,0:T(8,128)})) %all-reduce.8.cloned.1.call-update) | async-done | bytes 213008 | tf_op jit(solution)/shard_map/psum | solution.py:187
  362.6 247.8 %all-reduce.1 = (f32[128]{0:T(128)S(1)}, f32[128]{0:T(128)S(1)}, f32[128,14]{0,1:T(8,128)S(1)}, f32[14]{0:T(128)S(1)}, f32[]{:T(128)}) all-reduce(f32[128]{0:T(128)S(1)} %get-tuple-element.77, f32[128]{0:T(128)S(1)} %get-tuple-element.79, f32[128,14]{0,1:T(8,128)S(1)} %convolution_bitcast_fusion.1, ...), channel_id=1, replica_groups=mesh['dp'=4,'space'=64] {'space'}, use_global_device_ids=true, to_apply=%region_10.11 | all-reduce | flops 2063 | bytes 16504 | tf_op jit(solution)/shard_map/psum | solution.py:187
  610.4 15.1 %all-reduce.3 = (f32[128]{0:T(128)}, f32[128]{0:T(128)}, f32[128,14]{0,1:T(8,128)}, f32[14]{0:T(128)}, f32[]{:T(128)}) all-reduce(f32[128]{0:T(128)S(1)} %get-tuple-element.48, f32[128]{0:T(128)S(1)} %get-tuple-element.49, f32[128,14]{0,1:T(8,128)S(1)} %get-tuple-element.50, ...), channel_id=1, replica_groups=mesh['dp'=4,'space'=64] {'dp'}, use_global_device_ids=true, to_apply=%region_11.12 | all-reduce | flops 2063 | bytes 16504 | tf_op jit(solution)/shard_map/psum | solution.py:186
  626.1 1.6 copy.102
  (90 shorter events, 26.7 us)
Async XLA Ops:
  7.2 88.1 %copy-start = (bf16[3,3,32,128]{3,2,1,0:T(8,128)(2,1)S(1)}, bf16[3,3,32,128]{3,2,1,0:T(8,128)(2,1)}, u32[]{:S(2)}) copy-start(bf16[3,3,32,128]{3,2,1,0:T(8,128)(2,1)} %param.16) | copy-start | bytes 221188
  7.2 75.7 %copy-start.5 = (f32[1,14,192]{2,0,1:T(1,128)S(1)}, f32[1,14,192]{2,0,1:T(1,128)}, u32[]{:S(2)}) copy-start(f32[1,14,192]{2,0,1:T(1,128)} %param.15) | copy-start | bytes 32260
  8.7 83.3 %collective-permute-start = (bf16[1,32,1,128]{3,1,2,0:T(8,128)(2,1)S(1)}, bf16[1,32,1,128]{3,1,2,0:T(8,128)(2,1)S(1)}, u32[]{:S(2)}, u32[]{:S(2)}) collective-permute-start(bf16[1,32,1,128]{3,1,2,0:T(8,128)(2,1)S(1)} %get-tuple-element.68), channel_id=1, source_target_pairs={{0,1},{1,2},{2,3},{3,4},{4,5},{5,6},{6,7},{7,8},{8,9},{9,10},{10,1... | collective-permute-start | bytes 24584 | tf_op jit(solution)/shard_map/ppermute | solution.py:17
  10.4 81.5 %collective-permute-start.1 = (bf16[1,32,1,128]{3,1,2,0:T(8,128)(2,1)S(1)}, bf16[1,32,1,128]{3,1,2,0:T(8,128)(2,1)S(1)}, u32[]{:S(2)}, u32[]{:S(2)}) collective-permute-start(bf16[1,32,1,128]{3,1,2,0:T(8,128)(2,1)S(1)} %get-tuple-element.69), channel_id=1, source_target_pairs={{1,0},{2,1},{3,2},{4,3},{5,4},{6,5},{7,6},{8,7},{9,8},{10,9},{11,1... | collective-permute-start | bytes 24584 | tf_op jit(solution)/shard_map/ppermute | solution.py:20
  63.3 30.4 %copy-start.3 = (bf16[1,32,96,128]{3,2,1,0:T(8,128)(2,1)S(1)}, bf16[1,32,96,128]{3,2,1,0:T(8,128)(2,1)}, u32[]{:S(2)}) copy-start(bf16[1,32,96,128]{3,2,1,0:T(8,128)(2,1)} %param.11) | copy-start | bytes 2359300
  64.1 24.9 %all-to-all-start.1 = ((f32[1,1,64,3]{3,1,0,2:T(1,128)}), f32[1,1,64,3]{3,1,0,2:T(1,128)S(1)}, u32[]{:S(2)}, u32[]{:S(2)}) async-start(f32[1,1,64,3]{3,1,0,2:T(1,128)} %bitcast.12), calls=%async_computation.1 | async-start | bytes 65536 | tf_op jit(solution)/shard_map/all_to_all | solution.py:159
  95.3 2.9 copy-start.1
  98.2 2.8 copy-start.8
  98.2 2.8 copy-start.9
  98.2 2.8 copy-start.10
  100.9 6.2 copy-start.2
  100.9 6.2 copy-start.6
  101.0 6.2 copy-start.7
  126.5 15.2 %all-to-all-start = ((f32[1,14,64,3]{1,0,3,2:T(1,128)}), f32[1,14,64,3]{1,0,3,2:T(1,128)S(1)}, u32[]{:S(2)}, u32[]{:S(2)}) async-start(f32[1,14,64,3]{1,0,3,2:T(1,128)} %bitcast.79), calls=%async_computation | async-start | bytes 196608 | tf_op jit(solution)/shard_map/all_to_all | solution.py:152
  147.5 15.1 %all-to-all-start.2 = ((f32[1,14,64,3]{1,0,3,2:T(1,128)}), f32[1,14,64,3]{1,0,3,2:T(1,128)S(1)}, u32[]{:S(2)}, u32[]{:S(2)}) async-start(f32[1,14,64,3]{1,0,3,2:T(1,128)} %bitcast.80), calls=%async_computation.2 | async-start | bytes 196608 | tf_op jit(solution)/shard_map/all_to_all | solution.py:176
  152.0 209.0 %all-reduce.8.cloned.1.call-start = ((), (), s32[]{:S(2)}) async-start(), calls=%async_computation.3 | async-start | bytes 425984 | tf_op jit(solution)/shard_map/psum | solution.py:187
  173.8 8.8 %slice-start.2 = ((s8[6291456]{0:T(1024)(128)(4,1)}), s8[4194304]{0:T(1024)(128)(4,1)S(1)}, s32[]{:S(2)}) async-start(s8[6291456]{0:T(1024)(128)(4,1)} %bitcast.73), calls=%async_computation.7 | async-start | bytes 8388608
  175.7 6.9 %copy-start.4 = (bf16[14,96,128]{2,0,1:T(8,128)(2,1)}, bf16[14,96,128]{2,0,1:T(8,128)(2,1)S(1)}, u32[]{:S(2)}) copy-start(bf16[14,96,128]{2,0,1:T(8,128)(2,1)S(1)} %get-tuple-element.65) | copy-start | bytes 1032196
  175.7 6.9 %slice-start.3 = ((s8[6291456]{0:T(1024)(128)(4,1)}), s8[2097152]{0:T(1024)(128)(4,1)S(1)}, s32[]{:S(2)}) async-start(s8[6291456]{0:T(1024)(128)(4,1)} %bitcast.73), calls=%async_computation.8 | async-start | bytes 4194304
  175.7 14.8 %slice-start = ((s8[7077888]{0:T(1024)(128)(4,1)}), s8[4194304]{0:T(1024)(128)(4,1)S(1)}, s32[]{:S(2)}) async-start(s8[7077888]{0:T(1024)(128)(4,1)} %bitcast.71), calls=%async_computation.5 | async-start | bytes 8388608
  182.6 7.9 %slice-start.1 = ((s8[7077888]{0:T(1024)(128)(4,1)}), s8[2883584]{0:T(1024)(128)(4,1)S(1)}, s32[]{:S(2)}) async-start(s8[7077888]{0:T(1024)(128)(4,1)} %bitcast.71), calls=%async_computation.6 | async-start | bytes 5767168
  193.2 432.9 %all-reduce.10.cloned.1.call-start = ((), (), s32[]{:S(2)}) async-start(), calls=%async_computation.4 | async-start | bytes 425984 | tf_op jit(solution)/shard_map/psum | solution.py:186
Sparse Core Ops, SparseCore 0:
  193.3 167.6 all-reduce.7
  363.6 43.1 all-reduce.9
